TPU v7x, 256 devices: a whole 4x4x8 slice. The times are simulated.
256 devices in a mesh: tm: 64 (over x, z, core), space: 4 (over y).
Axes of the slice: x: 4, y: 4, z: 8, core: 2. Of those that a mesh axis runs over, the one named last changes fastest.
Arguments:
- snapshots: float32 [4096, 16384], P('tm', 'space'), as said below
- space_factor: float32 [16384, 256], P('space'), as said below
Outputs:
- time_factor: float32 [4096, 256], P('tm')
- loadings: float32 [256, 16384], P('tm', 'space')
Inputs may be any that keep to these rules, and one draw needn't show every extreme that they name: `snapshots`: entries are real values. `space_factor`: entries are real values; columns have norms between 0.05 and 1, the previous sweep's singular values.
All inputs are finite; a program needn't handle non-finite values.
Results may differ from a plain program's by a relative error of at most 0.0001.
Values sent between devices are 32-bit elements; how exact they have to be, the bound alone decides.
A program may use at most 64 MiB of HBM per device.

v0:
```python
import math
import jax
import jax.numpy as jnp
from jax import lax
from jax.sharding import PartitionSpec as P

RANK = 256
NS = 2


def inner(left, right):
    return lax.dot_general(
        left,
        right,
        (((0,), (0,)), ((), ())),
        precision=lax.Precision.HIGHEST,
        preferred_element_type=jnp.float32,
    )


def matmul(left, right):
    return jnp.dot(left, right, precision=lax.Precision.HIGHEST, preferred_element_type=jnp.float32)


def on_device(snapshots, space_factor):
    projected = lax.psum(matmul(snapshots, space_factor), "space")
    devices = lax.axis_size("tm")
    scaling = jnp.float32(math.sqrt(devices * snapshots.shape[0]))
    energy = lax.psum(jnp.sum(projected * projected), "tm")
    factor = projected / jnp.sqrt(energy)
    identity_mat = jnp.eye(RANK, dtype=jnp.float32)

    def advance(sweep, current):
        correlation = lax.psum(inner(current, current), "tm")
        return matmul(current, 1.5 * identity_mat - 0.5 * correlation)

    factor = lax.fori_loop(0, NS, advance, factor)
    loadings = lax.psum_scatter(inner(factor, snapshots), "tm", scatter_dimension=0, tiled=True)
    return (factor * scaling, loadings)


def solution(mesh):
    return jax.shard_map(
        on_device,
        mesh=mesh,
        in_specs=(P("tm", "space"), P("space", None)),
        out_specs=(P("tm", None), P("tm", "space")),
        check_vma=False,
    )
```

profile of v0, /device:TPU:8, one launch (start us, length us, event | category | flops | bytes accessed | tf_op | source)
XLA Modules:
  0.0 756.8 jit_solution(8482115746510413596)
XLA Ops:
  7.2 0.0 copy-start
  7.2 0.0 all-reduce.5.cloned.1.call-start
  7.2 1.2 copy-done
  8.4 5.1 fusion.10
  13.5 0.0 all-reduce.5.cloned.1.call-update
  13.5 48.2 %all-reduce.5.cloned.1.call-done = f32[64,256]{1,0:T(8,128)} async-done(((f32[64,256]{1,0:T(8,128)}), f32[64,256]{1,0:T(8,128)}) %all-reduce.5.cloned.1.call-update) | async-done | bytes 65552 | tf_op jit(solution)/shard_map/psum | solution.py:26
  61.7 1.5 multiply_reduce_fusion
  63.1 127.8 %psum.22 = f32[]{:T(128)} all-reduce(f32[]{:T(128)} %multiply_reduce_fusion), channel_id=1, replica_groups=mesh['tm'=64,'space'=4] {'tm'}, use_global_device_ids=true, to_apply=%region_2.0 | all-reduce | flops 1 | bytes 8 | tf_op jit(solution)/shard_map/psum | solution.py:29
  191.6 0.9 broadcast_divide_fusion
  192.5 356.2 %while.11 = (s32[]{:T(128)}, f32[64,256]{1,0:T(8,128)S(1)}, s32[]{:T(128)}) while((s32[]{:T(128)}, f32[64,256]{1,0:T(8,128)S(1)}, s32[]{:T(128)}) %tuple.25), condition=%wide.region_5.0_spmd.clone, body=%wide.region_3.0_spmd.clone.sunk | while | flops 100990976 | bytes 2424917 | solution.py:37
  192.5 0.0 all-reduce.9.cloned.1.call-start
  192.5 1.1 fusion.26
  193.7 0.0 all-reduce.9.cloned.1.call-update
  193.7 173.3 %all-reduce.9.cloned.1.call-done = f32[256,256]{1,0:T(8,128)} async-done(((f32[256,256]{1,0:T(8,128)}), f32[256,256]{1,0:T(8,128)}) %all-reduce.9.cloned.1.call-update) | async-done | bytes 262160 | tf_op jit(solution)/shard_map/while/body/eval_jaxpr/psum | solution.py:34
  366.9 1.3 convolution_bitcast_fusion.2
  368.2 0.0 all-reduce.9.cloned.1.call-start
  368.3 1.1 fusion.26
  369.4 0.0 all-reduce.9.cloned.1.call-update
  369.4 178.0 %all-reduce.9.cloned.1.call-done = f32[256,256]{1,0:T(8,128)} async-done(((f32[256,256]{1,0:T(8,128)}), f32[256,256]{1,0:T(8,128)}) %all-reduce.9.cloned.1.call-update) | async-done | bytes 262160 | tf_op jit(solution)/shard_map/while/body/eval_jaxpr/psum | solution.py:34
  547.4 1.3 convolution_bitcast_fusion.2
  548.7 0.0 all-reduce.7.cloned.1.call-start
  548.8 0.0 copy-start.1
  548.8 5.1 fusion.11
  553.9 0.0 all-reduce.7.cloned.1.call-update
  553.9 0.0 copy-done.1
  553.9 0.6 dynamic-slice
  555.2 0.6 broadcast_multiply_fusion
  555.8 192.9 %all-reduce.7.cloned.1.call-done = f32[256,4096]{1,0:T(8,128)} async-done(((f32[256,4096]{1,0:T(8,128)}), f32[256,4096]{1,0:T(8,128)}) %all-reduce.7.cloned.1.call-update) | async-done | bytes 4194320
  748.8 1.5 constant_dynamic-slice_fusion
  (2 shorter events, 0.0 us)
Async XLA Ops:
  7.2 1.2 copy-start
  7.2 54.5 %all-reduce.5.cloned.1.call-start = ((), (), s32[]{:S(2)}) async-start(), calls=%async_computation | async-start | bytes 131072 | tf_op jit(solution)/shard_map/psum | solution.py:26
  192.5 174.5 %all-reduce.9.cloned.1.call-start = ((), (), s32[]{:S(2)}) async-start(), calls=%async_computation.2 | async-start | bytes 524288 | tf_op jit(solution)/shard_map/while/body/eval_jaxpr/psum | solution.py:34
  368.2 179.2 %all-reduce.9.cloned.1.call-start = ((), (), s32[]{:S(2)}) async-start(), calls=%async_computation.2 | async-start | bytes 524288 | tf_op jit(solution)/shard_map/while/body/eval_jaxpr/psum | solution.py:34
  548.7 200.0 %all-reduce.7.cloned.1.call-start = ((), (), s32[]{:S(2)}) async-start(), calls=%async_computation.1 | async-start | bytes 8388608
  548.8 5.2 copy-start.1
Sparse Core Ops, SparseCore 0:
  13.6 48.0 all-reduce.4
  196.8 170.1 all-reduce.8
  372.5 174.8 all-reduce.8
  554.1 194.6 all-reduce.6
where the time goes:
time: 757 us
  waiting for transfers between devices  592 us (78%)
  blocking collectives  128 us (17%)
  between operations  15.1 us (2%)
  matrix products  15 us (2%)
    psum x2, waiting for transfers between devices, advance(): correlation = lax.psum(inner(current, current), 'tm')  351 us
    unnamed x3, waiting for transfers between devices  193 us
    psum x1, blocking collectives, on_device(): energy = lax.psum(jnp.sum(projected * projected), 'tm')  128 us
    psum x1, waiting for transfers between devices, on_device(): projected = lax.psum(matmul(snapshots, space_factor), 'space')  48.2 us
  transfers between devices with their start and end apart: 4, of which 4 were waited for; matrix products, arithmetic and copies ran while one was open for 0% of the time, Pallas kernels for 0%

commit v1 on v0

--- a/solution.py
+++ b/solution.py
@@ -23,7 +23,7 @@
 
 
 def on_device(snapshots, space_factor):
-    projected = lax.psum(matmul(snapshots, space_factor), "space")
+    projected = jnp.sum(lax.all_gather(matmul(snapshots, space_factor), "space"), axis=0)
     devices = lax.axis_size("tm")
     scaling = jnp.float32(math.sqrt(devices * snapshots.shape[0]))
     energy = lax.psum(jnp.sum(projected * projected), "tm")

time: 757 us -> 722 us (0.954)
  waiting for transfers between devices: 592 us -> 543 us
  blocking collectives: 128 us -> 142 us
    psum x1 -> x0, waiting for transfers between devices: 48.2 us -> none  [on_device(): projected = lax.psum(matmul(snapshots, space_factor), 'space')]
    all_gather x0 -> x1, blocking collectives: none -> 12.5 us  [on_device(): lax.all_gather(matmul(snapshots, space_factor), 'space')]
    unnamed x3 -> x2, waiting for transfers between devices: 193 us -> 193 us
  transfers between devices with their start and end apart: 4 -> 3, of which waited for: 4 -> 3; matrix products, arithmetic and copies ran while one was open for 0% -> 0% of each run, Pallas kernels for 0% -> 0%
where the time goes in v1:
time: 722 us; the launch traced here: 721 us
  waiting for transfers between devices  543 us (75%)
  blocking collectives  142 us (20%)
  between operations  16.8 us (2%)
  matrix products  14.3 us (2%)
    psum x2, waiting for transfers between devices, advance(): correlation = lax.psum(inner(current, current), 'tm')  351 us
    unnamed x2, waiting for transfers between devices  193 us
    psum x1, blocking collectives, on_device(): energy = lax.psum(jnp.sum(projected * projected), 'tm')  129 us
  transfers between devices with their start and end apart: 3, of which 3 were waited for; matrix products, arithmetic and copies ran while one was open for 0% of the time, Pallas kernels for 0%

profile of v1, /device:TPU:8, one launch (start us, length us, event | category | flops | bytes accessed | tf_op | source)
XLA Modules:
  0.0 721.2 jit_solution(15980828880150380366)
XLA Ops:
  8.0 0.0 copy-start
  8.0 1.2 copy-done
  9.2 4.4 fusion.10
  13.7 12.5 %all-gather = f32[256,256]{1,0:T(8,128)S(1)} all-gather(f32[64,256]{1,0:T(8,128)S(1)} %fusion.10), channel_id=2, replica_groups=mesh['tm'=64,'space'=4] {'space'}, dimensions={0}, use_global_device_ids=true | all-gather | bytes 327680 | tf_op jit(solution)/shard_map/all_gather | solution.py:26
  26.2 0.6 multiply_reduce_fusion
  26.8 129.2 %psum.14 = f32[]{:T(128)} all-reduce(f32[]{:T(128)} %multiply_reduce_fusion), channel_id=1, replica_groups=mesh['tm'=64,'space'=4] {'tm'}, use_global_device_ids=true, to_apply=%region_2.0 | all-reduce | flops 1 | bytes 8 | tf_op jit(solution)/shard_map/psum | solution.py:29
  156.7 355.6 %while.11 = (s32[]{:T(128)}, f32[64,256]{1,0:T(8,128)S(1)}, s32[]{:T(128)}) while((s32[]{:T(128)}, f32[64,256]{1,0:T(8,128)S(1)}, s32[]{:T(128)}) %tuple.25), condition=%wide.region_5.0_spmd.clone, body=%wide.region_3.0_spmd.clone.sunk | while | flops 100990976 | bytes 2424917 | solution.py:37
  156.8 0.0 all-reduce.6.cloned.1.call-start
  156.8 1.1 fusion.26
  157.9 0.0 all-reduce.6.cloned.1.call-update
  158.0 172.7 %all-reduce.6.cloned.1.call-done = f32[256,256]{1,0:T(8,128)} async-done(((f32[256,256]{1,0:T(8,128)}), f32[256,256]{1,0:T(8,128)}) %all-reduce.6.cloned.1.call-update) | async-done | bytes 262160 | tf_op jit(solution)/shard_map/while/body/eval_jaxpr/psum | solution.py:34
  330.6 1.3 convolution_bitcast_fusion.2
  331.9 0.0 all-reduce.6.cloned.1.call-start
  332.0 1.1 fusion.26
  333.1 0.0 all-reduce.6.cloned.1.call-update
  333.1 178.0 %all-reduce.6.cloned.1.call-done = f32[256,256]{1,0:T(8,128)} async-done(((f32[256,256]{1,0:T(8,128)}), f32[256,256]{1,0:T(8,128)}) %all-reduce.6.cloned.1.call-update) | async-done | bytes 262160 | tf_op jit(solution)/shard_map/while/body/eval_jaxpr/psum | solution.py:34
  511.1 1.3 convolution_bitcast_fusion.2
  512.4 0.0 all-reduce.4.cloned.1.call-start
  512.4 0.0 copy-start.1
  512.5 5.1 fusion.11
  517.6 0.0 all-reduce.4.cloned.1.call-update
  517.6 0.0 copy-done.1
  517.6 0.6 dynamic-slice
  518.9 0.6 broadcast_multiply_fusion
  519.5 192.7 %all-reduce.4.cloned.1.call-done = f32[256,4096]{1,0:T(8,128)} async-done(((f32[256,4096]{1,0:T(8,128)}), f32[256,4096]{1,0:T(8,128)}) %all-reduce.4.cloned.1.call-update) | async-done | bytes 4194320
  712.2 1.5 constant_dynamic-slice_fusion
  (4 shorter events, 0.0 us)
Async XLA Ops:
  8.0 1.2 copy-start
  156.8 173.9 %all-reduce.6.cloned.1.call-start = ((), (), s32[]{:S(2)}) async-start(), calls=%async_computation.1 | async-start | bytes 524288 | tf_op jit(solution)/shard_map/while/body/eval_jaxpr/psum | solution.py:34
  331.9 179.2 %all-reduce.6.cloned.1.call-start = ((), (), s32[]{:S(2)}) async-start(), calls=%async_computation.1 | async-start | bytes 524288 | tf_op jit(solution)/shard_map/while/body/eval_jaxpr/psum | solution.py:34
  512.4 199.8 %all-reduce.4.cloned.1.call-start = ((), (), s32[]{:S(2)}) async-start(), calls=%async_computation | async-start | bytes 8388608
  512.4 5.2 copy-start.1
Sparse Core Ops, SparseCore 0:
  161.0 169.5 all-reduce.5
  336.2 174.8 all-reduce.5
Sparse Core Ops, SparseCore 1:
  517.7 194.4 all-reduce.3
